TPU v7x, 32 devices: a whole 2x2x4 slice. The times are simulated.
32 devices in a mesh: clips: 2 (over x), seq: 8 (over z, y), head: 2 (over core).
Axes of the slice: x: 2, y: 2, z: 4, core: 2. Of those that a mesh axis runs over, the one named last changes fastest.
Arguments:
- video_q: bfloat16 [2048, 2048], P(('clips', 'seq'), 'head'), parts along dimension 0, may hold values from -105 to 105
- video_k: bfloat16 [2048, 2048], P(('clips', 'seq'), 'head'), parts along dimension 0, may hold values from -5 to 5
- video_v: bfloat16 [2048, 2048], P(('clips', 'seq'), 'head'), parts along dimension 0, may hold values from -6 to 6
- audio_q: bfloat16 [512, 2048], P(('clips', 'seq'), 'head'), parts along dimension 0, may hold values from -105 to 105
- audio_k: bfloat16 [512, 2048], P(('clips', 'seq'), 'head'), parts along dimension 0, may hold values from -5 to 5
- audio_v: bfloat16 [512, 2048], P(('clips', 'seq'), 'head'), parts along dimension 0, may hold values from -6 to 6
- video_query_gain: float32 [2048], P('head'), may hold values from 1 to 2
- video_key_gain: float32 [2048], P('head'), may hold values from 1 to 2
- audio_query_gain: float32 [2048], P('head'), may hold values from 1 to 2
- audio_key_gain: float32 [2048], P('head'), may hold values from 1 to 2
Outputs:
- video_mixed: bfloat16 [2048, 2048], P(('clips', 'seq'), 'head'), parts along dimension 0
- audio_mixed: bfloat16 [512, 2048], P(('clips', 'seq'), 'head'), parts along dimension 0
There are 2 independent parts, one for each index of `clips`. A program takes and returns all parts, laid end to end along the dimension named above; an argument that names none is the same for every part. Nothing has to cross between parts.
All inputs are finite; a program needn't handle non-finite values.
Results may differ from a plain program's by a relative error of at most 0.02.
Values may be sent and summed in bfloat16 or wider, within the bound.
A program may use at most 128 MiB of HBM per device.

v0:
```python
import jax
import jax.numpy as jnp
from jax import lax
from jax.sharding import PartitionSpec as P

HEAD_DIM = 128


def normed(tokens, gain_row):
    count = tokens.shape[0]
    head_count = tokens.shape[1] // HEAD_DIM
    entries = tokens.astype(jnp.float32).reshape(count, head_count, HEAD_DIM)
    scaled = entries * lax.rsqrt(jnp.mean(entries * entries, axis=2, keepdims=True) + 1e-06)
    return (scaled.reshape(count, head_count * HEAD_DIM) * gain_row).astype(jnp.bfloat16)


def start_state(row_count, head_count):
    return (
        jnp.full((head_count, row_count), -1e30, jnp.float32),
        jnp.zeros((head_count, row_count), jnp.float32),
        jnp.zeros((row_count, head_count, HEAD_DIM), jnp.float32),
    )


def folding(queries, prepare):
    head_count = queries.shape[1]

    def fold_step(state_now, pieces, offset):
        key_rows, values = prepare(pieces)
        key_rows = key_rows.reshape(key_rows.shape[0], head_count, HEAD_DIM)
        values = values.reshape(values.shape[0], head_count, HEAD_DIM)
        scores = jnp.einsum(
            "qhd,khd->hqk", queries, key_rows, preferred_element_type=jnp.float32
        ) * HEAD_DIM ** (-0.5)
        running_max, row_total, accumulated = state_now
        new_max = jnp.maximum(running_max, jnp.max(scores, axis=2))
        rescale = jnp.exp(running_max - new_max)
        weights = jnp.exp(scores - new_max[:, :, None])
        row_total = jnp.sum(weights, axis=2)
        update = jnp.einsum(
            "hqk,khd->qhd", weights.astype(jnp.bfloat16), values, preferred_element_type=jnp.float32
        )
        accumulated = accumulated * rescale.T[:, :, None] + update
        return (new_max, row_total, accumulated)

    return fold_step


def finish(state_now):
    running_max, row_total, accumulated = state_now
    result = accumulated / row_total.T[:, :, None]
    return result.reshape(result.shape[0], result.shape[1] * HEAD_DIM)


def as_heads(tokens):
    return tokens.reshape(tokens.shape[0], tokens.shape[1] // HEAD_DIM, HEAD_DIM)


def keep_pair(pieces):
    return pieces


def per_device(
    video_q,
    video_k,
    video_v,
    audio_q,
    audio_k,
    audio_v,
    video_query_gain,
    video_key_gain,
    audio_query_gain,
    audio_key_gain,
):
    head_count = video_q.shape[1] // HEAD_DIM
    video_rows = video_q.shape[0]
    audio_rows = audio_q.shape[0]
    video_state = folding(as_heads(video_q), keep_pair)(
        start_state(video_rows, head_count),
        (
            lax.all_gather(video_k, "seq", axis=0, tiled=True),
            lax.all_gather(video_v, "seq", axis=0, tiled=True),
        ),
        jnp.int32(0),
    )
    video_self = finish(video_state).astype(jnp.bfloat16)
    audio_state = folding(as_heads(audio_q), keep_pair)(
        start_state(audio_rows, head_count),
        (
            lax.all_gather(audio_k, "seq", axis=0, tiled=True),
            lax.all_gather(audio_v, "seq", axis=0, tiled=True),
        ),
        jnp.int32(0),
    )
    audio_self = finish(audio_state).astype(jnp.bfloat16)
    audio_whole = lax.all_gather(audio_self, "seq", axis=0, tiled=True)
    video_queries = as_heads(normed(video_self, video_query_gain))
    cross_step = folding(video_queries, keep_pair)
    video_cross = finish(
        cross_step(
            start_state(video_rows, head_count),
            (normed(audio_whole, audio_key_gain), audio_whole),
            0,
        )
    )
    audio_queries = normed(audio_self, audio_query_gain)

    def prepare_video(shard_rows):
        return (normed(shard_rows, video_key_gain), shard_rows)

    audio_state_cross = folding(as_heads(audio_queries), prepare_video)(
        start_state(audio_rows, head_count),
        lax.all_gather(video_self, "seq", axis=0, tiled=True),
        jnp.int32(0),
    )
    audio_cross = finish(audio_state_cross)
    video_mixed = (video_self.astype(jnp.float32) + video_cross).astype(jnp.bfloat16)
    audio_mixed = (audio_self.astype(jnp.float32) + audio_cross).astype(jnp.bfloat16)
    return (video_mixed, audio_mixed)


def solution(mesh):
    in_specs = (
        P(("clips", "seq"), "head"),
        P(("clips", "seq"), "head"),
        P(("clips", "seq"), "head"),
        P(("clips", "seq"), "head"),
        P(("clips", "seq"), "head"),
        P(("clips", "seq"), "head"),
        P("head"),
        P("head"),
        P("head"),
        P("head"),
    )
    out_specs = (P(("clips", "seq"), "head"), P(("clips", "seq"), "head"))
    return jax.shard_map(
        per_device, mesh=mesh, in_specs=in_specs, out_specs=out_specs, check_vma=False
    )
```

profile of v0, /device:TPU:0, one launch (start us, length us, event | category | flops | bytes accessed | tf_op | source)
XLA Modules:
  0.0 207.1 jit_solution(10102442533477169547)
XLA Ops:
  7.2 0.0 copy-start
  7.2 0.0 all-gather.4.cloned.1.call-start
  7.2 1.8 copy.72
  9.0 0.0 all-gather.4.cloned.1.call-update
  9.1 0.0 all-gather.6.cloned.1.call-start
  9.1 0.7 all-gather.6.cloned.1.call-update
  9.8 0.0 all-gather.8.cloned.1.call-start
  9.9 34.0 %all_gather.20 = bf16[256,1024]{1,0:T(8,128)(2,1)S(1)} all-gather(bf16[32,1024]{1,0:T(8,128)(2,1)} %param.14), channel_id=1, replica_groups=mesh['clips'=2,'seq'=8,'head'=2] {'seq'}, dimensions={0}, use_global_device_ids=true | all-gather | bytes 589824 | tf_op jit(solution)/shard_map/all_gather | solution.py:90
  43.9 0.2 copy.76
  44.1 22.5 %all-gather.4.cloned.1.call-done = bf16[1024,1024]{0,1:T(8,128)(2,1)} async-done(((bf16[128,1024]{0,1:T(8,128)(2,1)}), bf16[1024,1024]{0,1:T(8,128)(2,1)}) %all-gather.4.cloned.1.call-update) | async-done | bytes 2097168 | tf_op jit(solution)/shard_map/all_gather | solution.py:81
  66.6 0.0 copy-done
  66.6 2.4 %multiply_reduce_fusion = (f32[8,128]{1,0:T(8,128)S(1)}, f32[8,128,1024]{2,1,0:T(8,128)S(1)}) fusion(bf16[1024,8,128]{0,2,1:T(8,128)(2,1)} %bitcast.127, bf16[128,1024]{1,0:T(8,128)(2,1)S(1)} %copy-done), kind=kOutput, calls=%fused_computation.6 | convolution fusion | flops 270531584 | bytes 6557696 | tf_op jit(solution)/shard_map/qhd,khd->hqk/dot_general | solution.py:32
  68.9 0.0 copy-start.2
  68.9 1.9 copy-done.2
  70.9 0.9 fusion.2
  71.8 44.2 %all-gather.6.cloned.1.call-done = bf16[1024,1024]{1,0:T(8,128)(2,1)} async-done(((bf16[128,1024]{1,0:T(8,128)(2,1)}), bf16[1024,1024]{1,0:T(8,128)(2,1)}) %all-gather.6.cloned.1.call-update) | async-done | bytes 2097168 | tf_op jit(solution)/shard_map/all_gather | solution.py:82
  116.0 2.9 %copy.75 = bf16[1024,1024]{0,1:T(8,128)(2,1)S(1)} copy(bf16[1024,1024]{1,0:T(8,128)(2,1)} %all-gather.6.cloned.1.call-done) | data formatting | bytes 4194304 | tf_op jit(solution)/shard_map/all_gather | solution.py:82
  118.8 0.0 copy-start.4
  118.9 0.0 copy-start.5
  118.9 4.2 %fusion.35 = (f32[128,8]{0,1:T(8,128)S(1)}, bf16[128,8,128]{0,2,1:T(8,128)(2,1)}) fusion(f32[128,8]{0,1:T(8,128)S(1)} %bitcast.135, bf16[1024,8,128]{0,2,1:T(8,128)(2,1)S(1)} %bitcast.125, f32[8,128,1024]{2,1,0:T(8,128)} %copy-done.2, f32[8,128]{1,0:T(8,128)S(1)} %get-tuple-element.15, f32[128,8]{0,1:T(8,128)S(1)} %get-tuple-element.14), kind=kOutput, calls=%fused_computation.43 | convolution fusion | flops 272366592 | bytes 6569984 | tf_op jit(solution)/shard_map/hqk,khd->qhd/dot_general | solution.py:40
  123.0 0.0 all-gather.8.cloned.1.call-update
  123.0 0.0 copy-done.4
  123.1 32.6 %all_gather.21 = bf16[256,1024]{1,0:T(8,128)(2,1)S(1)} all-gather(bf16[32,1024]{1,0:T(8,128)(2,1)S(1)} %copy-done.4), channel_id=1, replica_groups=mesh['clips'=2,'seq'=8,'head'=2] {'seq'}, dimensions={0}, use_global_device_ids=true | all-gather | bytes 589824 | tf_op jit(solution)/shard_map/all_gather | solution.py:91
  155.7 0.2 copy.79
  155.9 0.0 copy-done.5
  155.9 0.3 fusion.66
  156.2 0.2 fusion.52
  156.4 0.4 fusion.54
  156.8 0.0 copy-start.3
  156.8 0.0 copy-start.6
  156.8 0.0 copy-start.7
  156.9 32.9 %all_gather.22 = bf16[256,1024]{1,0:T(8,128)(2,1)S(1)} all-gather(bf16[32,1024]{1,0:T(8,128)(2,1)S(1)} %copy_bitcast_fusion), channel_id=1, replica_groups=mesh['clips'=2,'seq'=8,'head'=2] {'seq'}, dimensions={0}, use_global_device_ids=true | all-gather | bytes 589824 | tf_op jit(solution)/shard_map/all_gather | solution.py:96
  189.8 0.2 copy.86
  190.0 0.1 fusion.22
  190.1 0.2 copy.102
  190.3 0.3 reduce_sum.75
  190.7 0.1 copy.82
  190.7 0.1 copy.83
  190.9 0.3 mul.152
  191.3 0.0 copy-done.3
  191.3 0.0 copy-done.6
  191.3 0.0 copy-done.7
  191.3 0.7 fusion.67
  192.0 0.0 copy-start.8
  192.0 0.4 fusion.31
  192.4 0.4 fusion.12
  192.8 0.0 copy-start.9
  192.8 0.1 fusion.43
  192.9 0.9 copy.90
  193.7 0.0 all-gather.8.cloned.1.call-done
  193.7 2.1 bitcast_reduce_fusion
  195.8 0.0 copy-done.8
  195.8 0.0 copy-start.1
  195.9 2.3 %fusion.1 = bf16[1024,1024]{0,1:T(8,128)(2,1)S(1)} fusion(bf16[1024,1024]{0,1:T(8,128)(2,1)} %all-gather.8.cloned.1.call-done, f32[1024]{0:T(1024)S(1)} %copy-done.8, f32[1024,8]{0,1:T(8,128)S(1)} %add_rsqrt_fusion), kind=kLoop, calls=%fused_computation.3 | loop fusion | flops 4194304 | bytes 4231168 | tf_op jit(solution)/shard_map/convert_element_type | solution.py:14
  198.1 0.0 copy-done.9
  198.1 0.5 fusion.68
  198.7 0.3 fusion.33
  199.0 0.0 copy-done.1
  199.0 0.9 fusion.18
  199.9 0.7 fusion.58
  (9 shorter events, 0.1 us)
Async XLA Ops:
  7.2 59.4 %copy-start = (bf16[128,1024]{1,0:T(8,128)(2,1)S(1)}, bf16[128,1024]{1,0:T(8,128)(2,1)}, u32[]{:S(2)}) copy-start(bf16[128,1024]{1,0:T(8,128)(2,1)} %param.10) | copy-start | bytes 786436
  7.2 59.4 %all-gather.4.cloned.1.call-start = ((), (), s32[]{:S(2)}) async-start(), calls=%async_computation | async-start | bytes 2359296 | tf_op jit(solution)/shard_map/all_gather | solution.py:81
  9.1 106.9 %all-gather.6.cloned.1.call-start = ((), (), s32[]{:S(2)}) async-start(), calls=%async_computation.1 | async-start | bytes 2359296 | tf_op jit(solution)/shard_map/all_gather | solution.py:82
  9.8 183.9 %all-gather.8.cloned.1.call-start = ((), (), s32[]{:S(2)}) async-start(), calls=%async_computation.2 | async-start | bytes 2359296 | tf_op jit(solution)/shard_map/all_gather | solution.py:113
  68.9 1.9 copy-start.2
  118.8 4.2 %copy-start.4 = (bf16[32,1024]{1,0:T(8,128)(2,1)S(1)}, bf16[32,1024]{1,0:T(8,128)(2,1)}, u32[]{:S(2)}) copy-start(bf16[32,1024]{1,0:T(8,128)(2,1)} %param.15) | copy-start | bytes 196612
  118.9 37.0 %copy-start.5 = (bf16[32,1024]{1,0:T(8,128)(2,1)S(1)}, bf16[32,1024]{1,0:T(8,128)(2,1)}, u32[]{:S(2)}) copy-start(bf16[32,1024]{1,0:T(8,128)(2,1)} %param.13) | copy-start | bytes 196612
  156.8 34.4 %copy-start.3 = (bf16[128,8,128]{0,2,1:T(8,128)(2,1)S(1)}, bf16[128,8,128]{0,2,1:T(8,128)(2,1)}, u32[]{:S(2)}) copy-start(bf16[128,8,128]{0,2,1:T(8,128)(2,1)} %get-tuple-element.23) | copy-start | bytes 786436
  156.8 34.4 %copy-start.6 = (f32[1024]{0:T(1024)S(1)}, f32[1024]{0:T(1024)}, u32[]{:S(2)}) copy-start(f32[1024]{0:T(1024)} %param.16) | copy-start | bytes 12292
  156.8 34.4 %copy-start.7 = (f32[1024]{0:T(1024)S(1)}, f32[1024]{0:T(1024)}, u32[]{:S(2)}) copy-start(f32[1024]{0:T(1024)} %param.19) | copy-start | bytes 12292
  192.0 3.9 %copy-start.8 = (f32[1024]{0:T(1024)S(1)}, f32[1024]{0:T(1024)}, u32[]{:S(2)}) copy-start(f32[1024]{0:T(1024)} %param.17) | copy-start | bytes 12292
  192.8 5.3 %copy-start.9 = (f32[1024]{0:T(1024)S(1)}, f32[1024]{0:T(1024)}, u32[]{:S(2)}) copy-start(f32[1024]{0:T(1024)} %param.18) | copy-start | bytes 12292
  195.8 3.2 %copy-start.1 = (bf16[1024,1024]{0,1:T(8,128)(2,1)S(1)}, bf16[1024,1024]{0,1:T(8,128)(2,1)}, u32[]{:S(2)}) copy-start(bf16[1024,1024]{0,1:T(8,128)(2,1)} %all-gather.8.cloned.1.call-done) | copy-start | bytes 6291460
Sparse Core Ops, SparseCore 0:
  10.6 55.9 all-gather.3
  68.7 47.2 all-gather.5
  123.2 58.0 all-gather.7
where the time goes:
time: 207 us
  blocking collectives  99.6 us (48%)
  waiting for transfers between devices  67.4 us (33%)
  between operations  14.1 us (7%)
  matrix products  9.72 us (5%)
  local copies, waits for them, and re-layouts  8.84 us (4%)
  other arithmetic  7.4 us (4%)
    all_gather x1, waiting for transfers between devices, per_device(): lax.all_gather(video_v, 'seq', axis=0, tiled=True)  44.2 us
    all_gather x1, blocking collectives, per_device(): lax.all_gather(audio_k, 'seq', axis=0, tiled=True)  34 us
    all_gather x1, blocking collectives, per_device(): audio_whole = lax.all_gather(audio_self, 'seq', axis=0, tiled=True)  32.9 us
    all_gather x1, blocking collectives, per_device(): lax.all_gather(audio_v, 'seq', axis=0, tiled=True)  32.6 us
    all_gather x1, waiting for transfers between devices, per_device(): lax.all_gather(video_k, 'seq', axis=0, tiled=True)  22.5 us
    dot_general x4, matrix products, fold_step(): jnp.einsum('hqk,khd->qhd', weights.astype(jnp.bfloat16), values, preferre...  5.84 us
    unnamed x23, local copies, waits for them, and re-layouts  4.84 us
  transfers between devices with their start and end apart: 3, of which 2 were waited for; matrix products, arithmetic and copies ran while one was open for 4% of the time, Pallas kernels for 0%

commit v1 on v0

--- a/solution.py
+++ b/solution.py
@@ -1,9 +1,15 @@
+import functools
+import math
+
 import jax
 import jax.numpy as jnp
 from jax import lax
+from jax.experimental import pallas as pl
+from jax.experimental.pallas import tpu as pltpu
 from jax.sharding import PartitionSpec as P
 
 HEAD_DIM = 128
+EXP2_SCALE = HEAD_DIM ** (-0.5) * math.log2(math.e)
 
 
 def normed(tokens, gain_row):
@@ -119,6 +125,291 @@
     return (video_mixed, audio_mixed)
 
 
+def attend_kernel(
+    n,
+    video_q,
+    video_k,
+    video_v,
+    audio_q,
+    audio_k,
+    audio_v,
+    video_query_gain,
+    video_key_gain,
+    audio_query_gain,
+    audio_key_gain,
+    video_out,
+    audio_out,
+    vq,
+    vk,
+    vv,
+    aq,
+    ak,
+    av,
+    video_self,
+    audio_self,
+    audio_queries,
+    audio_keys,
+    audio_sum,
+    video_mixed,
+    audio_mixed,
+    send_sem,
+    recv_sem,
+    own_sem,
+    out_send_sem,
+    out_recv_sem,
+    out_own_sem,
+):
+    me = lax.axis_index("seq")
+    rows = video_q.shape[0]
+    arows = audio_q.shape[0]
+
+    def peer_of(step, sign):
+        distance = lax.select(step % 2 == 1, (step + 1) // 2, n - step // 2)
+        return lax.rem(me + n + sign * distance, n)
+
+    def head_columns(index):
+        return pl.ds(pl.multiple_of(index * HEAD_DIM, HEAD_DIM), HEAD_DIM)
+
+    def token_rows(index, count):
+        return pl.ds(pl.multiple_of(index * count, count), count)
+
+    ins = (
+        (audio_k, ak, arows),
+        (audio_v, av, arows),
+        (audio_q, aq, arows),
+        (video_k, vk, rows),
+        (video_v, vv, rows),
+        (video_q, vq, rows),
+    )
+
+    def own_in(kind):
+        source, target, count = ins[kind]
+        return pltpu.make_async_copy(
+            source.at[:, head_columns(me)],
+            target.at[token_rows(me, count), pl.ds(0, HEAD_DIM)],
+            own_sem.at[kind],
+        )
+
+    def sent_in(kind, peer):
+        source, target, count = ins[kind]
+        return pltpu.make_async_remote_copy(
+            src_ref=source.at[:, head_columns(peer)],
+            dst_ref=target.at[token_rows(me, count), pl.ds(0, HEAD_DIM)],
+            send_sem=send_sem.at[kind, peer],
+            recv_sem=recv_sem.at[kind, me],
+            device_id={"seq": peer},
+            device_id_type=pl.DeviceIdType.MESH,
+        )
+
+    def received_in(kind, peer):
+        source, target, count = ins[kind]
+        return pltpu.make_async_remote_copy(
+            src_ref=source.at[:, head_columns(peer)],
+            dst_ref=target.at[token_rows(peer, count), pl.ds(0, HEAD_DIM)],
+            send_sem=send_sem.at[kind, peer],
+            recv_sem=recv_sem.at[kind, peer],
+            device_id={"seq": peer},
+            device_id_type=pl.DeviceIdType.MESH,
+        )
+
+    outs = ((audio_mixed, audio_out, arows), (video_mixed, video_out, rows))
+
+    def own_out(kind):
+        source, target, count = outs[kind]
+        return pltpu.make_async_copy(
+            source.at[token_rows(me, count), :],
+            target.at[:, head_columns(me)],
+            out_own_sem.at[kind],
+        )
+
+    def sent_out(kind, peer):
+        source, target, count = outs[kind]
+        return pltpu.make_async_remote_copy(
+            src_ref=source.at[token_rows(peer, count), :],
+            dst_ref=target.at[:, head_columns(me)],
+            send_sem=out_send_sem.at[kind, peer],
+            recv_sem=out_recv_sem.at[kind, me],
+            device_id={"seq": peer},
+            device_id_type=pl.DeviceIdType.MESH,
+        )
+
+    def received_out(kind, peer):
+        source, target, count = outs[kind]
+        return pltpu.make_async_remote_copy(
+            src_ref=source.at[token_rows(peer, count), :],
+            dst_ref=target.at[:, head_columns(peer)],
+            send_sem=out_send_sem.at[kind, peer],
+            recv_sem=out_recv_sem.at[kind, peer],
+            device_id={"seq": peer},
+            device_id_type=pl.DeviceIdType.MESH,
+        )
+
+    for kind in range(len(ins)):
+        own_in(kind).start()
+
+    barrier = pltpu.get_barrier_semaphore()
+    for step in range(1, n):
+        pl.semaphore_signal(
+            barrier,
+            inc=1,
+            device_id={"seq": lax.rem(me + step, n)},
+            device_id_type=pl.DeviceIdType.MESH,
+        )
+    pl.semaphore_wait(barrier, n - 1)
+
+    for kinds in SEND_ORDER:
+
+        def send_step(step, carry, kinds=kinds):
+            for kind in kinds:
+                sent_in(kind, peer_of(step, 1)).start()
+            return carry
+
+        lax.fori_loop(1, n, send_step, 0)
+
+    ones = jnp.ones((arows * n, HEAD_DIM), jnp.bfloat16)
+    av[:, HEAD_DIM:] = ones
+    audio_self[:, HEAD_DIM:] = ones
+    ones = jnp.ones((rows * n, HEAD_DIM), jnp.bfloat16)
+    vv[:, HEAD_DIM:] = ones
+    video_self[:, HEAD_DIM:] = ones
+    audio_sum[...] = jnp.zeros_like(audio_sum)
+
+    def wait_kinds(kinds):
+        for kind in kinds:
+            own_in(kind).wait()
+
+        def wait_step(step, carry):
+            for kind in kinds:
+                received_in(kind, peer_of(step, -1)).wait_recv()
+            return carry
+
+        lax.fori_loop(1, n, wait_step, 0)
+
+    def dot_t(left, right):
+        return lax.dot_general(
+            left, right, (((1,), (1,)), ((), ())), preferred_element_type=jnp.float32
+        )
+
+    def dot(left, right):
+        return jnp.dot(left, right, preferred_element_type=jnp.float32)
+
+    def self_attend(queries, key_rows, values):
+        scores = dot_t(queries, key_rows)
+        largest = jnp.max(scores, axis=1, keepdims=True)
+        weights = jnp.exp2((scores - largest) * EXP2_SCALE).astype(jnp.bfloat16)
+        both = dot(weights, values)
+        return (both[:, :HEAD_DIM] / both[:, HEAD_DIM:]).astype(jnp.bfloat16)
+
+    def unit(tokens):
+        entries = tokens.astype(jnp.float32)
+        mean = jnp.mean(entries * entries, axis=1, keepdims=True)
+        return entries * lax.rsqrt(mean + 1e-06)
+
+    own_head = pl.ds(me, 1)
+    wait_kinds((0, 1, 2))
+    tokens = self_attend(aq[...], ak[...], av[...])
+    audio_self[:, :HEAD_DIM] = tokens
+    scaled = unit(tokens)
+    audio_queries[...] = (scaled * audio_query_gain[own_head, :]).astype(jnp.bfloat16)
+    audio_keys[...] = (scaled * audio_key_gain[own_head, :]).astype(jnp.bfloat16)
+
+    wait_kinds((3, 4))
+
+    def video_block(peer):
+        here = token_rows(peer, rows)
+        tokens = self_attend(vq[here, :], vk[...], vv[...])
+        video_self[here, :HEAD_DIM] = tokens
+        scaled = unit(tokens)
+        queries = (scaled * video_query_gain[own_head, :]).astype(jnp.bfloat16)
+        key_rows = (scaled * video_key_gain[own_head, :]).astype(jnp.bfloat16)
+        weights = jnp.exp2(dot_t(queries, audio_keys[...]) * EXP2_SCALE)
+        both = dot(weights.astype(jnp.bfloat16), audio_self[...])
+        cross = both[:, :HEAD_DIM] / both[:, HEAD_DIM:]
+        video_mixed[here, :] = (tokens.astype(jnp.float32) + cross).astype(jnp.bfloat16)
+        weights = jnp.exp2(dot_t(audio_queries[...], key_rows) * EXP2_SCALE)
+        audio_sum[...] += dot(weights.astype(jnp.bfloat16), video_self[here, :])
+
+    own_in(5).wait()
+    video_block(me)
+    own_out(1).start()
+
+    def block_step(step, carry):
+        peer = peer_of(step, -1)
+        received_in(5, peer).wait_recv()
+        video_block(peer)
+        sent_out(1, peer).start()
+        return carry
+
+    lax.fori_loop(1, n, block_step, 0)
+
+    both = audio_sum[...]
+    cross = both[:, :HEAD_DIM] / both[:, HEAD_DIM:]
+    audio_mixed[...] = (audio_self[:, :HEAD_DIM].astype(jnp.float32) + cross).astype(jnp.bfloat16)
+    own_out(0).start()
+
+    def send_audio(step, carry):
+        sent_out(0, peer_of(step, 1)).start()
+        return carry
+
+    lax.fori_loop(1, n, send_audio, 0)
+
+    def finish_step(step, carry):
+        peer = peer_of(step, 1)
+        for kind in range(len(ins)):
+            sent_in(kind, peer).wait_send()
+        for kind in range(len(outs)):
+            sent_out(kind, peer).wait_send()
+            received_out(kind, peer).wait_recv()
+        return carry
+
+    lax.fori_loop(1, n, finish_step, 0)
+    own_out(0).wait()
+    own_out(1).wait()
+
+
+SEND_ORDER = ((0, 1, 2), (3, 4), (5,))
+
+
+def head_per_device(n, *arrays):
+    video_q, audio_q = arrays[0], arrays[3]
+    tokens, atokens = video_q.shape[0] * n, audio_q.shape[0] * n
+    bf16, f32 = jnp.bfloat16, jnp.float32
+    gains = [gain.reshape(n, HEAD_DIM) for gain in arrays[6:]]
+    anywhere = pl.BlockSpec(memory_space=pl.ANY)
+    vmem = pl.BlockSpec(memory_space=pltpu.VMEM)
+    return pl.pallas_call(
+        functools.partial(attend_kernel, n),
+        out_shape=(
+            jax.ShapeDtypeStruct(video_q.shape, bf16),
+            jax.ShapeDtypeStruct(audio_q.shape, bf16),
+        ),
+        in_specs=[anywhere] * 6 + [vmem] * 4,
+        out_specs=(anywhere, anywhere),
+        scratch_shapes=[
+            pltpu.VMEM((tokens, HEAD_DIM), bf16),
+            pltpu.VMEM((tokens, HEAD_DIM), bf16),
+            pltpu.VMEM((tokens, 2 * HEAD_DIM), bf16),
+            pltpu.VMEM((atokens, HEAD_DIM), bf16),
+            pltpu.VMEM((atokens, HEAD_DIM), bf16),
+            pltpu.VMEM((atokens, 2 * HEAD_DIM), bf16),
+            pltpu.VMEM((tokens, 2 * HEAD_DIM), bf16),
+            pltpu.VMEM((atokens, 2 * HEAD_DIM), bf16),
+            pltpu.VMEM((atokens, HEAD_DIM), bf16),
+            pltpu.VMEM((atokens, HEAD_DIM), bf16),
+            pltpu.VMEM((atokens, 2 * HEAD_DIM), f32),
+            pltpu.VMEM((tokens, HEAD_DIM), bf16),
+            pltpu.VMEM((atokens, HEAD_DIM), bf16),
+            pltpu.SemaphoreType.DMA((6, n)),
+            pltpu.SemaphoreType.DMA((6, n)),
+            pltpu.SemaphoreType.DMA((6,)),
+            pltpu.SemaphoreType.DMA((2, n)),
+            pltpu.SemaphoreType.DMA((2, n)),
+            pltpu.SemaphoreType.DMA((2,)),
+        ],
+        compiler_params=pltpu.CompilerParams(collective_id=0, has_side_effects=True),
+    )(*arrays[:6], *gains)
+
+
 def solution(mesh):
     in_specs = (
         P(("clips", "seq"), "head"),
@@ -133,6 +424,18 @@
         P("head"),
     )
     out_specs = (P(("clips", "seq"), "head"), P(("clips", "seq"), "head"))
+    sizes = dict(mesh.shape)
+
+    def body(*arrays):
+        video_q, audio_q = arrays[0], arrays[3]
+        if (
+            video_q.shape[1] == sizes["seq"] * HEAD_DIM
+            and video_q.shape[0] % 16 == 0
+            and audio_q.shape[0] % 16 == 0
+        ):
+            return head_per_device(sizes["seq"], *arrays)
+        return per_device(*arrays)
+
     return jax.shard_map(
-        per_device, mesh=mesh, in_specs=in_specs, out_specs=out_specs, check_vma=False
-    )
+        body, mesh=mesh, in_specs=in_specs, out_specs=out_specs, check_vma=False
+    )

time: 207 us -> 44.8 us (0.22)
  blocking collectives: 99.6 us -> 0 us
  waiting for transfers between devices: 67.4 us -> 0 us
  Pallas kernels: 0 us -> 41.6 us
  between operations: 14.1 us -> 0.65 us
  matrix products: 9.72 us -> 0 us
  other arithmetic: 7.4 us -> 0 us
  local copies, waits for them, and re-layouts: 8.84 us -> 2.33 us
    all_gather x3 -> x0, blocking collectives: 99.6 us -> none  [the longest x1 34 us: per_device(): lax.all_gather(audio_k, 'seq', axis=0, tiled=True)]
    all_gather x3 -> x0, waiting for transfers between devices: 66.7 us -> none  [the longest x1 44.2 us: per_device(): lax.all_gather(video_v, 'seq', axis=0, tiled=True)]
    pallas_call x0 -> x1, Pallas kernels: none -> 41.6 us  [head_per_device(): pl.pallas_call(functools.partial(attend_kernel, n), out_shape=(jax.ShapeD...]
    dot_general x8 -> x0, matrix products: 9.72 us -> none  [the longest x4 5.84 us: fold_step(): jnp.einsum('hqk,khd->qhd', weights.astype(jnp.bfloat16), values, preferre...]
    reduce_sum x6 -> x0, other arithmetic: 4.22 us -> none  [the longest x2 2.41 us: normed(): jnp.mean(entries * entries, axis=2, keepdims=True) + 1e-06]
    all_gather x4 -> x0, local copies, waits for them, and re-layouts: 3.46 us -> none  [the longest x1 2.85 us: per_device(): lax.all_gather(video_v, 'seq', axis=0, tiled=True)]
    convert_element_type x3 -> x0, other arithmetic: 3 us -> none  [the longest x1 2.26 us: normed(): (scaled.reshape(count, head_count * HEAD_DIM) * gain_row).astype(jnp.bflo...]
    unnamed x23 -> x4, local copies, waits for them, and re-layouts: 4.84 us -> 2.33 us
  transfers between devices with their start and end apart: 3 -> 0, of which waited for: 2 -> 0; matrix products, arithmetic and copies ran while one was open for 4% -> 0% of each run, Pallas kernels for 0% -> 0%
where the time goes in v1:
time: 44.8 us; the launch traced here: 44.6 us
  Pallas kernels  41.6 us (93%)
  local copies, waits for them, and re-layouts  2.33 us (5%)
  between operations  0.65 us (1%)
    pallas_call x1, Pallas kernels, head_per_device(): pl.pallas_call(functools.partial(attend_kernel, n), out_shape=(jax.ShapeD...  41.6 us
    unnamed x4, local copies, waits for them, and re-layouts  2.33 us

profile of v1, /device:TPU:0, one launch (start us, length us, event | category | flops | bytes accessed | tf_op | source)
XLA Modules:
  0.0 44.6 jit_solution(3845036993596126367)
XLA Ops:
  0.6 41.6 %shard_map.113 = (bf16[128,1024]{1,0:T(8,128)(2,1)}, bf16[32,1024]{1,0:T(8,128)(2,1)}) custom-call(bf16[128,1024]{1,0:T(8,128)(2,1)} %video_q.1, bf16[128,1024]{1,0:T(8,128)(2,1)} %video_k.1, bf16[128,1024]{1,0:T(8,128)(2,1)} %video_v.1, bf16[32,1024]{1,0:T(8,128)(2,1)} %audio_q.1, bf16[32,1024]{1,0:T(8,128)(2,1)} %audio_k.1, bf16[32,1024]{1,0:T(8,128)(2,1)} %audio_v.1, ...), custom_call_target="tpu_custom_call" | custom-call | tf_op jit(solution)/shard_map/pallas_call | solution.py:380
  42.3 0.0 copy-start
  42.3 1.7 %copy.14 = bf16[128,1024]{1,0:T(8,128)(2,1)} copy(bf16[128,1024]{1,0:T(8,128)(2,1)} %get-tuple-element.4) | data formatting | bytes 524288
  44.0 0.0 copy-done
  44.0 0.6 %copy.15 = bf16[32,1024]{1,0:T(8,128)(2,1)} copy(bf16[32,1024]{1,0:T(8,128)(2,1)S(1)} %copy-done) | data formatting | bytes 131072
Async XLA Ops:
  42.3 1.7 %copy-start = (bf16[32,1024]{1,0:T(8,128)(2,1)S(1)}, bf16[32,1024]{1,0:T(8,128)(2,1)}, u32[]{:S(2)}) copy-start(bf16[32,1024]{1,0:T(8,128)(2,1)} %get-tuple-element.5) | copy-start | bytes 196612

commit v2 on v1

--- a/solution.py
+++ b/solution.py
@@ -145,7 +145,6 @@
     aq,
     ak,
     av,
-    video_self,
     audio_self,
     audio_queries,
     audio_keys,
@@ -163,9 +162,29 @@
     rows = video_q.shape[0]
     arows = audio_q.shape[0]
 
-    def peer_of(step, sign):
-        distance = lax.select(step % 2 == 1, (step + 1) // 2, n - step // 2)
-        return lax.rem(me + n + sign * distance, n)
+    half = n // 2 if n % 2 == 0 else n
+    far_count = n - half
+
+    def near_peer(step, sign):
+        return me // half * half + lax.rem(lax.rem(me, half) + half + sign * step, half)
+
+    def far_peer(step, sign):
+        return lax.rem(near_peer(step, sign) + half, n)
+
+    def over_peers(visit, sign, far_first):
+        def far(step, carry):
+            visit(far_peer(step, sign))
+            return carry
+
+        def near(step, carry):
+            visit(near_peer(step, sign))
+            return carry
+
+        if far_first:
+            lax.fori_loop(0, far_count, far, 0)
+        lax.fori_loop(1, half, near, 0)
+        if not far_first:
+            lax.fori_loop(0, far_count, far, 0)
 
     def head_columns(index):
         return pl.ds(pl.multiple_of(index * HEAD_DIM, HEAD_DIM), HEAD_DIM)
@@ -257,33 +276,30 @@
         )
     pl.semaphore_wait(barrier, n - 1)
 
-    for kinds in SEND_ORDER:
-
-        def send_step(step, carry, kinds=kinds):
+    for kinds, far_first in SEND_ORDER:
+
+        def send_kinds(peer, kinds=kinds):
             for kind in kinds:
-                sent_in(kind, peer_of(step, 1)).start()
-            return carry
-
-        lax.fori_loop(1, n, send_step, 0)
+                sent_in(kind, peer).start()
+
+        over_peers(send_kinds, 1, far_first)
 
     ones = jnp.ones((arows * n, HEAD_DIM), jnp.bfloat16)
     av[:, HEAD_DIM:] = ones
     audio_self[:, HEAD_DIM:] = ones
     ones = jnp.ones((rows * n, HEAD_DIM), jnp.bfloat16)
     vv[:, HEAD_DIM:] = ones
-    video_self[:, HEAD_DIM:] = ones
     audio_sum[...] = jnp.zeros_like(audio_sum)
 
     def wait_kinds(kinds):
         for kind in kinds:
             own_in(kind).wait()
 
-        def wait_step(step, carry):
+        def wait_peer(peer):
             for kind in kinds:
-                received_in(kind, peer_of(step, -1)).wait_recv()
-            return carry
-
-        lax.fori_loop(1, n, wait_step, 0)
+                received_in(kind, peer).wait_recv()
+
+        over_peers(wait_peer, -1, False)
 
     def dot_t(left, right):
         return lax.dot_general(
@@ -315,59 +331,101 @@
 
     wait_kinds((3, 4))
 
-    def video_block(peer):
-        here = token_rows(peer, rows)
-        tokens = self_attend(vq[here, :], vk[...], vv[...])
-        video_self[here, :HEAD_DIM] = tokens
+    def self_part(peers):
+        here = [token_rows(peer, rows) for peer in peers]
+        tokens = self_attend(jnp.concatenate([vq[one, :] for one in here], 0), vk[...], vv[...])
         scaled = unit(tokens)
         queries = (scaled * video_query_gain[own_head, :]).astype(jnp.bfloat16)
         key_rows = (scaled * video_key_gain[own_head, :]).astype(jnp.bfloat16)
+        return tokens, queries, key_rows
+
+    def audio_part(tokens, key_rows):
+        weights = jnp.exp2(dot_t(audio_queries[...], key_rows) * EXP2_SCALE)
+        values = jnp.concatenate([tokens, jnp.ones_like(tokens)], 1)
+        audio_sum[...] += dot(weights.astype(jnp.bfloat16), values)
+
+    def video_part(peers, tokens, queries):
         weights = jnp.exp2(dot_t(queries, audio_keys[...]) * EXP2_SCALE)
         both = dot(weights.astype(jnp.bfloat16), audio_self[...])
         cross = both[:, :HEAD_DIM] / both[:, HEAD_DIM:]
-        video_mixed[here, :] = (tokens.astype(jnp.float32) + cross).astype(jnp.bfloat16)
-        weights = jnp.exp2(dot_t(audio_queries[...], key_rows) * EXP2_SCALE)
-        audio_sum[...] += dot(weights.astype(jnp.bfloat16), video_self[here, :])
-
-    own_in(5).wait()
-    video_block(me)
-    own_out(1).start()
-
-    def block_step(step, carry):
-        peer = peer_of(step, -1)
-        received_in(5, peer).wait_recv()
-        video_block(peer)
-        sent_out(1, peer).start()
-        return carry
-
-    lax.fori_loop(1, n, block_step, 0)
-
-    both = audio_sum[...]
-    cross = both[:, :HEAD_DIM] / both[:, HEAD_DIM:]
-    audio_mixed[...] = (audio_self[:, :HEAD_DIM].astype(jnp.float32) + cross).astype(jnp.bfloat16)
-    own_out(0).start()
-
-    def send_audio(step, carry):
-        sent_out(0, peer_of(step, 1)).start()
-        return carry
-
-    lax.fori_loop(1, n, send_audio, 0)
-
-    def finish_step(step, carry):
-        peer = peer_of(step, 1)
+        mixed = (tokens.astype(jnp.float32) + cross).astype(jnp.bfloat16)
+        for index, peer in enumerate(peers):
+            video_mixed[token_rows(peer, rows), :] = mixed[index * rows : (index + 1) * rows]
+
+    def send_audio(peer):
+        sent_out(0, peer).start()
+
+    others = [far_peer(step, -1) for step in range(far_count)]
+    others += [near_peer(step, -1) for step in range(1, half)]
+    group = GROUP if n % GROUP == 0 else 1
+    for first in range(0, n, group):
+        last = first + group == n
+        here = others[first : first + group]
+        for peer in here:
+            received_in(5, peer).wait_recv()
+        if last:
+            own_in(5).wait()
+        peers = here + [me] if last else here
+        tokens, queries, key_rows = self_part(peers)
+        if not last:
+            video_part(peers, tokens, queries)
+            for peer in here:
+                sent_out(1, peer).start()
+            audio_part(tokens, key_rows)
+        else:
+            audio_part(tokens, key_rows)
+            both = audio_sum[...]
+            cross = both[:, :HEAD_DIM] / both[:, HEAD_DIM:]
+            audio_mixed[...] = (
+                audio_self[:, :HEAD_DIM].astype(jnp.float32) + cross
+            ).astype(jnp.bfloat16)
+            own_out(0).start()
+            over_peers(send_audio, 1, True)
+            video_part(peers, tokens, queries)
+            for peer in here:
+                sent_out(1, peer).start()
+            own_out(1).start()
+
+    def finish_peer(peer):
         for kind in range(len(ins)):
             sent_in(kind, peer).wait_send()
         for kind in range(len(outs)):
             sent_out(kind, peer).wait_send()
             received_out(kind, peer).wait_recv()
-        return carry
-
-    lax.fori_loop(1, n, finish_step, 0)
+
+    over_peers(finish_peer, 1, True)
     own_out(0).wait()
     own_out(1).wait()
 
 
-SEND_ORDER = ((0, 1, 2), (3, 4), (5,))
+def pass_on_kernel(
+    video_in, audio_in, video_out, audio_out, video_held, audio_held, in_sem, out_sem
+):
+    loads, stores = [], []
+    for kind, (source, held, target) in enumerate(
+        ((video_in, video_held, video_out), (audio_in, audio_held, audio_out))
+    ):
+        piece = source.shape[1] // PIECES
+        for index in range(PIECES):
+            here = (slice(None), pl.ds(index * piece, piece))
+            loads.append(
+                pltpu.make_async_copy(source.at[here], held.at[here], in_sem.at[kind, index])
+            )
+            stores.append(
+                pltpu.make_async_copy(held.at[here], target.at[here], out_sem.at[kind, index])
+            )
+    for load in loads:
+        load.start()
+    for load, store in zip(loads, stores):
+        load.wait()
+        store.start()
+    for store in stores:
+        store.wait()
+
+
+PIECES = 2
+GROUP = 2
+SEND_ORDER = (((0, 1, 2), False), ((3, 4), False), ((5,), True))
 
 
 def head_per_device(n, *arrays):
@@ -377,7 +435,7 @@
     gains = [gain.reshape(n, HEAD_DIM) for gain in arrays[6:]]
     anywhere = pl.BlockSpec(memory_space=pl.ANY)
     vmem = pl.BlockSpec(memory_space=pltpu.VMEM)
-    return pl.pallas_call(
+    results = pl.pallas_call(
         functools.partial(attend_kernel, n),
         out_shape=(
             jax.ShapeDtypeStruct(video_q.shape, bf16),
@@ -392,7 +450,6 @@
             pltpu.VMEM((atokens, HEAD_DIM), bf16),
             pltpu.VMEM((atokens, HEAD_DIM), bf16),
             pltpu.VMEM((atokens, 2 * HEAD_DIM), bf16),
-            pltpu.VMEM((tokens, 2 * HEAD_DIM), bf16),
             pltpu.VMEM((atokens, 2 * HEAD_DIM), bf16),
             pltpu.VMEM((atokens, HEAD_DIM), bf16),
             pltpu.VMEM((atokens, HEAD_DIM), bf16),
@@ -408,6 +465,21 @@
         ],
         compiler_params=pltpu.CompilerParams(collective_id=0, has_side_effects=True),
     )(*arrays[:6], *gains)
+    return pl.pallas_call(
+        pass_on_kernel,
+        out_shape=(
+            jax.ShapeDtypeStruct(video_q.shape, bf16),
+            jax.ShapeDtypeStruct(audio_q.shape, bf16),
+        ),
+        in_specs=[anywhere] * 2,
+        out_specs=(anywhere, anywhere),
+        scratch_shapes=[
+            pltpu.VMEM(video_q.shape, bf16),
+            pltpu.VMEM(audio_q.shape, bf16),
+            pltpu.SemaphoreType.DMA((2, PIECES)),
+            pltpu.SemaphoreType.DMA((2, PIECES)),
+        ],
+    )(*results)
 
 
 def solution(mesh):

time: 44.8 us -> 42.2 us (0.942)
  local copies, waits for them, and re-layouts: 2.33 us -> 0 us
    unnamed x4 -> x0, local copies, waits for them, and re-layouts: 2.33 us -> none
    pallas_call x1, Pallas kernels: 41.6 us -> 39.7 us  [head_per_device(): pl.pallas_call(functools.partial(attend_kernel, n), out_shape=(jax.ShapeD...]
    pallas_call x0 -> x1, Pallas kernels: none -> 1.71 us  [head_per_device(): pl.pallas_call(pass_on_kernel, out_shape=(jax.ShapeDtypeStruct(video_q.sh...]
where the time goes in v2:
time: 42.2 us; the launch traced here: 42 us
  Pallas kernels  41.4 us (98%)
  between operations  0.64 us (2%)
    pallas_call x1, Pallas kernels, head_per_device(): pl.pallas_call(functools.partial(attend_kernel, n), out_shape=(jax.ShapeD...  39.7 us
    pallas_call x1, Pallas kernels, head_per_device(): pl.pallas_call(pass_on_kernel, out_shape=(jax.ShapeDtypeStruct(video_q.sh...  1.71 us

profile of v2, /device:TPU:0, one launch (start us, length us, event | category | flops | bytes accessed | tf_op | source)
XLA Modules:
  0.0 42.0 jit_solution(8147468945293659988)
XLA Ops:
  0.6 39.7 %shard_map.113 = (bf16[128,1024]{1,0:T(8,128)(2,1)}, bf16[32,1024]{1,0:T(8,128)(2,1)}) custom-call(bf16[128,1024]{1,0:T(8,128)(2,1)} %video_q.1, bf16[128,1024]{1,0:T(8,128)(2,1)} %video_k.1, bf16[128,1024]{1,0:T(8,128)(2,1)} %video_v.1, bf16[32,1024]{1,0:T(8,128)(2,1)} %audio_q.1, bf16[32,1024]{1,0:T(8,128)(2,1)} %audio_k.1, bf16[32,1024]{1,0:T(8,128)(2,1)} %audio_v.1, ...), custom_call_target="tpu_custom_call" | custom-call | tf_op jit(solution)/shard_map/pallas_call | solution.py:438
  40.3 1.7 %shard_map.114 = (bf16[128,1024]{1,0:T(8,128)(2,1)}, bf16[32,1024]{1,0:T(8,128)(2,1)}) custom-call(bf16[128,1024]{1,0:T(8,128)(2,1)} %get-tuple-element.4.video_in, bf16[32,1024]{1,0:T(8,128)(2,1)} %get-tuple-element.5.audio_in), custom_call_target="tpu_custom_call" | custom-call | tf_op jit(solution)/shard_map/pallas_call | solution.py:468

commit v3 on v2

--- a/solution.py
+++ b/solution.py
@@ -157,6 +157,7 @@
     out_send_sem,
     out_recv_sem,
     out_own_sem,
+    far_in_sem,
 ):
     me = lax.axis_index("seq")
     rows = video_q.shape[0]
@@ -266,23 +267,33 @@
     for kind in range(len(ins)):
         own_in(kind).start()
 
+    def signal(semaphore, peer):
+        pl.semaphore_signal(
+            semaphore,
+            inc=1,
+            device_id={"seq": peer},
+            device_id_type=pl.DeviceIdType.MESH,
+        )
+
+    def send(kinds, peers):
+        for kind in kinds:
+            for peer in peers:
+                sent_in(kind, peer).start()
+
     barrier = pltpu.get_barrier_semaphore()
-    for step in range(1, n):
-        pl.semaphore_signal(
-            barrier,
-            inc=1,
-            device_id={"seq": lax.rem(me + step, n)},
-            device_id_type=pl.DeviceIdType.MESH,
-        )
-    pl.semaphore_wait(barrier, n - 1)
-
-    for kinds, far_first in SEND_ORDER:
-
-        def send_kinds(peer, kinds=kinds):
-            for kind in kinds:
-                sent_in(kind, peer).start()
-
-        over_peers(send_kinds, 1, far_first)
+    near = [near_peer(step, 1) for step in range(1, half)]
+    far = [far_peer(step, 1) for step in range(far_count)]
+    for peer in far[:1] + near:
+        signal(barrier, peer)
+    pl.semaphore_wait(barrier, len(far[:1] + near))
+    for peer in near:
+        signal(far_in_sem, peer)
+    for kinds, which in EARLY_ORDER:
+        send(kinds, near if which == "near" else far[:1])
+    if near:
+        pl.semaphore_wait(far_in_sem, len(near))
+    for kinds, which in LATE_ORDER:
+        send(kinds, {"near": near, "rest": far[1:], "far": far}[which])
 
     ones = jnp.ones((arows * n, HEAD_DIM), jnp.bfloat16)
     av[:, HEAD_DIM:] = ones
@@ -425,7 +436,8 @@
 
 PIECES = 2
 GROUP = 2
-SEND_ORDER = (((0, 1, 2), False), ((3, 4), False), ((5,), True))
+EARLY_ORDER = (((0, 1, 2), "first"), ((0, 1, 2), "near"), ((3, 4), "first"), ((3, 4), "near"))
+LATE_ORDER = (((0, 1, 2), "rest"), ((3, 4), "rest"), ((5,), "far"), ((5,), "near"))
 
 
 def head_per_device(n, *arrays):
@@ -462,6 +474,7 @@
             pltpu.SemaphoreType.DMA((2, n)),
             pltpu.SemaphoreType.DMA((2, n)),
             pltpu.SemaphoreType.DMA((2,)),
+            pltpu.SemaphoreType.REGULAR,
         ],
         compiler_params=pltpu.CompilerParams(collective_id=0, has_side_effects=True),
     )(*arrays[:6], *gains)

time: 42.2 us -> 41 us (0.972)
  Pallas kernels: 41.4 us -> 40.2 us
    pallas_call x1, Pallas kernels: 39.7 us -> 38.5 us  [head_per_device(): pl.pallas_call(functools.partial(attend_kernel, n), out_shape=(jax.ShapeD...]
where the time goes in v3:
time: 41 us; the launch traced here: 40.8 us
  Pallas kernels  40.2 us (98%)
  between operations  0.64 us (2%)
    pallas_call x1, Pallas kernels, head_per_device(): pl.pallas_call(functools.partial(attend_kernel, n), out_shape=(jax.ShapeD...  38.5 us
    pallas_call x1, Pallas kernels, head_per_device(): pl.pallas_call(pass_on_kernel, out_shape=(jax.ShapeDtypeStruct(video_q.sh...  1.71 us

profile of v3, /device:TPU:0, one launch (start us, length us, event | category | flops | bytes accessed | tf_op | source)
XLA Modules:
  0.0 40.8 jit_solution(17782977905759303094)
XLA Ops:
  0.6 38.5 %shard_map.113 = (bf16[128,1024]{1,0:T(8,128)(2,1)}, bf16[32,1024]{1,0:T(8,128)(2,1)}) custom-call(bf16[128,1024]{1,0:T(8,128)(2,1)} %video_q.1, bf16[128,1024]{1,0:T(8,128)(2,1)} %video_k.1, bf16[128,1024]{1,0:T(8,128)(2,1)} %video_v.1, bf16[32,1024]{1,0:T(8,128)(2,1)} %audio_q.1, bf16[32,1024]{1,0:T(8,128)(2,1)} %audio_k.1, bf16[32,1024]{1,0:T(8,128)(2,1)} %audio_v.1, ...), custom_call_target="tpu_custom_call" | custom-call | tf_op jit(solution)/shard_map/pallas_call | solution.py:450
  39.1 1.7 %shard_map.114 = (bf16[128,1024]{1,0:T(8,128)(2,1)}, bf16[32,1024]{1,0:T(8,128)(2,1)}) custom-call(bf16[128,1024]{1,0:T(8,128)(2,1)} %get-tuple-element.4.video_in, bf16[32,1024]{1,0:T(8,128)(2,1)} %get-tuple-element.5.audio_in), custom_call_target="tpu_custom_call" | custom-call | tf_op jit(solution)/shard_map/pallas_call | solution.py:481

commit v4 on v3

--- a/solution.py
+++ b/solution.py
@@ -133,10 +133,10 @@
     audio_q,
     audio_k,
     audio_v,
-    video_query_gain,
-    video_key_gain,
-    audio_query_gain,
-    audio_key_gain,
+    video_query_gain_in,
+    video_key_gain_in,
+    audio_query_gain_in,
+    audio_key_gain_in,
     video_out,
     audio_out,
     vq,
@@ -158,6 +158,11 @@
     out_recv_sem,
     out_own_sem,
     far_in_sem,
+    video_query_gain,
+    video_key_gain,
+    audio_query_gain,
+    audio_key_gain,
+    gain_sem,
 ):
     me = lax.axis_index("seq")
     rows = video_q.shape[0]
@@ -263,9 +268,6 @@
             device_id={"seq": peer},
             device_id_type=pl.DeviceIdType.MESH,
         )
-
-    for kind in range(len(ins)):
-        own_in(kind).start()
 
     def signal(semaphore, peer):
         pl.semaphore_signal(
@@ -295,6 +297,22 @@
     for kinds, which in LATE_ORDER:
         send(kinds, {"near": near, "rest": far[1:], "far": far}[which])
 
+    gains = [
+        pltpu.make_async_copy(source, target, gain_sem.at[index])
+        for index, (source, target) in enumerate(
+            (
+                (video_query_gain_in, video_query_gain),
+                (video_key_gain_in, video_key_gain),
+                (audio_query_gain_in, audio_query_gain),
+                (audio_key_gain_in, audio_key_gain),
+            )
+        )
+    ]
+    for gain in gains:
+        gain.start()
+    for kind in range(len(ins)):
+        own_in(kind).start()
+
     ones = jnp.ones((arows * n, HEAD_DIM), jnp.bfloat16)
     av[:, HEAD_DIM:] = ones
     audio_self[:, HEAD_DIM:] = ones
@@ -333,6 +351,8 @@
         return entries * lax.rsqrt(mean + 1e-06)
 
     own_head = pl.ds(me, 1)
+    for gain in gains:
+        gain.wait()
     wait_kinds((0, 1, 2))
     tokens = self_attend(aq[...], ak[...], av[...])
     audio_self[:, :HEAD_DIM] = tokens
@@ -409,33 +429,19 @@
     own_out(1).wait()
 
 
-def pass_on_kernel(
-    video_in, audio_in, video_out, audio_out, video_held, audio_held, in_sem, out_sem
-):
-    loads, stores = [], []
-    for kind, (source, held, target) in enumerate(
-        ((video_in, video_held, video_out), (audio_in, audio_held, audio_out))
-    ):
-        piece = source.shape[1] // PIECES
-        for index in range(PIECES):
-            here = (slice(None), pl.ds(index * piece, piece))
-            loads.append(
-                pltpu.make_async_copy(source.at[here], held.at[here], in_sem.at[kind, index])
-            )
-            stores.append(
-                pltpu.make_async_copy(held.at[here], target.at[here], out_sem.at[kind, index])
-            )
-    for load in loads:
-        load.start()
-    for load, store in zip(loads, stores):
-        load.wait()
-        store.start()
-    for store in stores:
-        store.wait()
-
-
-PIECES = 2
+def pass_on_kernel(video_in, audio_in, video_out, audio_out, sem):
+    copies = (
+        pltpu.make_async_copy(video_in, video_out, sem.at[0]),
+        pltpu.make_async_copy(audio_in, audio_out, sem.at[1]),
+    )
+    for copy in copies:
+        copy.start()
+    for copy in copies:
+        copy.wait()
+
+
 GROUP = 2
+KERNEL_BYTES = 24 * 2**20
 EARLY_ORDER = (((0, 1, 2), "first"), ((0, 1, 2), "near"), ((3, 4), "first"), ((3, 4), "near"))
 LATE_ORDER = (((0, 1, 2), "rest"), ((3, 4), "rest"), ((5,), "far"), ((5,), "near"))
 
@@ -446,14 +452,16 @@
     bf16, f32 = jnp.bfloat16, jnp.float32
     gains = [gain.reshape(n, HEAD_DIM) for gain in arrays[6:]]
     anywhere = pl.BlockSpec(memory_space=pl.ANY)
-    vmem = pl.BlockSpec(memory_space=pltpu.VMEM)
+    operands = [
+        pltpu.with_memory_space_constraint(one, pltpu.HBM) for one in (*arrays[:6], *gains)
+    ]
     results = pl.pallas_call(
         functools.partial(attend_kernel, n),
         out_shape=(
             jax.ShapeDtypeStruct(video_q.shape, bf16),
             jax.ShapeDtypeStruct(audio_q.shape, bf16),
         ),
-        in_specs=[anywhere] * 6 + [vmem] * 4,
+        in_specs=[anywhere] * 10,
         out_specs=(anywhere, anywhere),
         scratch_shapes=[
             pltpu.VMEM((tokens, HEAD_DIM), bf16),
@@ -475,9 +483,13 @@
             pltpu.SemaphoreType.DMA((2, n)),
             pltpu.SemaphoreType.DMA((2,)),
             pltpu.SemaphoreType.REGULAR,
+            *[pltpu.VMEM((n, HEAD_DIM), f32)] * 4,
+            pltpu.SemaphoreType.DMA((4,)),
         ],
-        compiler_params=pltpu.CompilerParams(collective_id=0, has_side_effects=True),
-    )(*arrays[:6], *gains)
+        compiler_params=pltpu.CompilerParams(
+            collective_id=0, has_side_effects=True, vmem_limit_bytes=KERNEL_BYTES
+        ),
+    )(*operands)
     return pl.pallas_call(
         pass_on_kernel,
         out_shape=(
@@ -486,12 +498,8 @@
         ),
         in_specs=[anywhere] * 2,
         out_specs=(anywhere, anywhere),
-        scratch_shapes=[
-            pltpu.VMEM(video_q.shape, bf16),
-            pltpu.VMEM(audio_q.shape, bf16),
-            pltpu.SemaphoreType.DMA((2, PIECES)),
-            pltpu.SemaphoreType.DMA((2, PIECES)),
-        ],
+        scratch_shapes=[pltpu.SemaphoreType.DMA((2,))],
+        compiler_params=pltpu.CompilerParams(vmem_limit_bytes=KERNEL_BYTES // 4),
     )(*results)
 
 

time: 41 us -> 39.3 us (0.959)
  Pallas kernels: 40.2 us -> 38.4 us
    pallas_call x1, Pallas kernels: 1.71 us -> 0.74 us  [head_per_device(): pl.pallas_call(pass_on_kernel, out_shape=(jax.ShapeDtypeStruct(video_q.sh...]
    pallas_call x1, Pallas kernels: 38.5 us -> 37.7 us  [head_per_device(): pl.pallas_call(functools.partial(attend_kernel, n), out_shape=(jax.ShapeD...]
where the time goes in v4:
time: 39.3 us; the launch traced here: 39.1 us
  Pallas kernels  38.4 us (98%)
  between operations  0.64 us (2%)
    pallas_call x1, Pallas kernels, head_per_device(): pl.pallas_call(functools.partial(attend_kernel, n), out_shape=(jax.ShapeD...  37.7 us

profile of v4, /device:TPU:0, one launch (start us, length us, event | category | flops | bytes accessed | tf_op | source)
XLA Modules:
  0.0 39.1 jit_solution(15402943215523013998)
XLA Ops:
  0.6 37.7 %shard_map.113 = (bf16[128,1024]{1,0:T(8,128)(2,1)S(1)}, bf16[32,1024]{1,0:T(8,128)(2,1)S(1)}) custom-call(bf16[128,1024]{1,0:T(8,128)(2,1)} %video_q.1, bf16[128,1024]{1,0:T(8,128)(2,1)} %video_k.1, bf16[128,1024]{1,0:T(8,128)(2,1)} %video_v.1, bf16[32,1024]{1,0:T(8,128)(2,1)} %audio_q.1, bf16[32,1024]{1,0:T(8,128)(2,1)} %audio_k.1, ...), custom_call_target="tpu_custom_call" | custom-call | tf_op jit(solution)/shard_map/pallas_call | solution.py:458
  38.3 0.7 %shard_map.114 = (bf16[128,1024]{1,0:T(8,128)(2,1)}, bf16[32,1024]{1,0:T(8,128)(2,1)}) custom-call(bf16[128,1024]{1,0:T(8,128)(2,1)S(1)} %get-tuple-element.4.video_in, bf16[32,1024]{1,0:T(8,128)(2,1)S(1)} %get-tuple-element.5.audio_in), custom_call_target="tpu_custom_call" | custom-call | tf_op jit(solution)/shard_map/pallas_call | solution.py:493

commit v5 on v4

--- a/solution.py
+++ b/solution.py
@@ -443,7 +443,7 @@
 GROUP = 2
 KERNEL_BYTES = 24 * 2**20
 EARLY_ORDER = (((0, 1, 2), "first"), ((0, 1, 2), "near"), ((3, 4), "first"), ((3, 4), "near"))
-LATE_ORDER = (((0, 1, 2), "rest"), ((3, 4), "rest"), ((5,), "far"), ((5,), "near"))
+LATE_ORDER = (((0, 1, 2), "rest"), ((3, 4), "rest"), ((5,), "near"), ((5,), "far"))
 
 
 def head_per_device(n, *arrays):

time: 39.3 us -> 39.3 us (level)
  no operation moved by 1% of the time
where the time goes in v5:
time: 39.3 us; the launch traced here: 39.1 us
  Pallas kernels  38.4 us (98%)
  between operations  0.64 us (2%)
    pallas_call x1, Pallas kernels, head_per_device(): pl.pallas_call(functools.partial(attend_kernel, n), out_shape=(jax.ShapeD...  37.7 us

profile of v5, /device:TPU:0, one launch (start us, length us, event | category | flops | bytes accessed | tf_op | source)
XLA Modules:
  0.0 39.1 jit_solution(4303016397021004794)
XLA Ops:
  0.6 37.7 %shard_map.113 = (bf16[128,1024]{1,0:T(8,128)(2,1)S(1)}, bf16[32,1024]{1,0:T(8,128)(2,1)S(1)}) custom-call(bf16[128,1024]{1,0:T(8,128)(2,1)} %video_q.1, bf16[128,1024]{1,0:T(8,128)(2,1)} %video_k.1, bf16[128,1024]{1,0:T(8,128)(2,1)} %video_v.1, bf16[32,1024]{1,0:T(8,128)(2,1)} %audio_q.1, bf16[32,1024]{1,0:T(8,128)(2,1)} %audio_k.1, ...), custom_call_target="tpu_custom_call" | custom-call | tf_op jit(solution)/shard_map/pallas_call | solution.py:458
  38.3 0.7 %shard_map.114 = (bf16[128,1024]{1,0:T(8,128)(2,1)}, bf16[32,1024]{1,0:T(8,128)(2,1)}) custom-call(bf16[128,1024]{1,0:T(8,128)(2,1)S(1)} %get-tuple-element.4.video_in, bf16[32,1024]{1,0:T(8,128)(2,1)S(1)} %get-tuple-element.5.audio_in), custom_call_target="tpu_custom_call" | custom-call | tf_op jit(solution)/shard_map/pallas_call | solution.py:493
